TPU v7x, 128 devices: a whole 4x4x4 slice. The times are simulated.
128 devices in a mesh: ka: 32 (over y, z, core), gz: 4 (over x).
Axes of the slice: x: 4, y: 4, z: 4, core: 2. Of those that a mesh axis runs over, the one named last changes fastest.
Arguments:
- fields: float32 [32, 2, 32, 3, 25600], P('ka', None, None, None, 'gz'), may hold values from -0.25 to 0.25
- bvectors: float32 [2, 3], replicated, may hold values from -0.5 to 0.5
- gshift: int32 [32, 2, 3], replicated, may hold values from -1 to 1
Outputs:
- intersections: float32 [32, 4, 2, 32, 32], P('ka')
All inputs are finite; a program needn't handle non-finite values.
Results may differ from a plain program's by a relative error of at most 0.0003.
Values sent between devices are 32-bit elements; how exact they have to be, the bound alone decides.
A program may use at most 128 MiB of HBM per device.

v0:
```python
import math

import jax
import jax.numpy as jnp
from jax import lax
from jax.experimental import pallas as pl
from jax.experimental.pallas import tpu as pltpu
from jax.sharding import PartitionSpec as P

GX = 40
GY = 40
NZ = 16
ROW = 8
ROWS = 4
SLOTS = 12
TILES = 6
HALF = 3
LANES = 128
MESH = pl.DeviceIdType.MESH
TWO_PI = 2.0 * math.pi


def split(value):
    high = value.astype(jnp.bfloat16)
    low = (value - high.astype(jnp.float32)).astype(jnp.bfloat16)
    return high, low


def contract(left, right):
    return lax.dot_general(
        left, right, (((1,), (1,)), ((), ())), preferred_element_type=jnp.float32
    )


def kernel(
    bvec_ref, gshift_ref, field_ref, out_ref,
    buf, xbuf, phase, acc, stage, reduced, total, gathered,
    send_sem, recv_sem, xsend_sem, xrecv_sem, fsend_sem, xfsend_sem,
    rsend_sem, rrecv_sem, gsend_sem, grecv_sem, rows_sem,
):
    me = lax.axis_index("ka")
    gx = lax.axis_index("gz")
    row = me // ROW
    own = me % ROW
    zpos = own // 2
    core = own % 2
    row_up = (row + 1) % ROWS
    row_down = (row + ROWS - 1) % ROWS

    def at(r, j):
        return {"ka": r * ROW + j}

    def peer(dz, dc):
        return ((zpos + dz) % 4) * 2 + (core + dc) % 2

    peers = [peer(2, 0), peer(2, 1), peer(1, 0), peer(3, 0), peer(1, 1), peer(3, 1), peer(0, 1)]

    barrier = pltpu.get_barrier_semaphore()
    for p in peers:
        pl.semaphore_signal(barrier, inc=1, device_id=at(row, p), device_id_type=MESH)
    for r in (row_up, row_down):
        pl.semaphore_signal(barrier, inc=1, device_id=at(r, own), device_id_type=MESH)
    for dx in (1, 2, 3):
        pl.semaphore_signal(barrier, inc=1, device_id={"gz": (gx + dx) % 4}, device_id_type=MESH)
    pl.semaphore_wait(barrier, 12)

    def extra_source(p):
        comp = jnp.minimum(p // 2, 2)
        start = pl.multiple_of((ROW * TILES + p % 2) * LANES, LANES)
        return field_ref.at[:, comp, :, pl.ds(start, LANES)]

    def tile_source(p, t):
        start = pl.multiple_of((p * TILES + t) * LANES, LANES)
        return field_ref.at[:, :, :, pl.ds(start, LANES)]

    for p in peers:
        pltpu.make_async_remote_copy(
            src_ref=extra_source(p), dst_ref=xbuf.at[own],
            send_sem=xsend_sem, recv_sem=xrecv_sem.at[own // 4],
            device_id=at(row, p), device_id_type=MESH,
        ).start()
    pltpu.make_async_copy(extra_source(own), xbuf.at[own], xrecv_sem.at[own // 4]).start()

    def send_tile(n, carry):
        t = (n + HALF * (zpos // 2)) % TILES
        shift = t // HALF
        slot = t * SLOTS + own + 4 * shift
        group = own // 4 + shift
        for p in peers:
            pltpu.make_async_remote_copy(
                src_ref=tile_source(p, t), dst_ref=buf.at[slot],
                send_sem=send_sem.at[t], recv_sem=recv_sem.at[t, group],
                device_id=at(row, p), device_id_type=MESH,
            ).start()
        pltpu.make_async_copy(tile_source(own, t), buf.at[slot], recv_sem.at[t, group]).start()
        return carry

    lax.fori_loop(0, TILES, send_tile, 0)

    for r in (row_up, row_down):
        pl.semaphore_signal(rows_sem, inc=1, device_id=at(r, own), device_id_type=MESH)

    row_id = lax.broadcasted_iota(jnp.int32, (16, LANES), 0)
    lane = lax.broadcasted_iota(jnp.int32, (16, LANES), 1).astype(jnp.float32)

    def q_rows(h):
        parts = []
        for a in range(3):
            q = jnp.zeros((16, LANES), jnp.float32)
            for d in range(2):
                for i in range(8):
                    k = (row * ROW + i - 4 * h + 32) % 32
                    value = bvec_ref[d, a] + gshift_ref[a, d, k].astype(jnp.float32)
                    q = jnp.where(row_id == d * 8 + i, value, q)
            parts.append(q)
        return parts

    def write_phase(index, q, start, keep):
        cell = lane + start.astype(jnp.float32)
        line = jnp.floor((cell + 0.5) * (1.0 / GX))
        plane = jnp.floor((cell + 0.5) * (1.0 / (GX * GY)))
        xc = cell - GX * line
        yc = line - GY * plane
        zc = plane + (gx * 4).astype(jnp.float32)
        theta = -TWO_PI * (q[0] * xc / GX + q[1] * yc / GY + q[2] * zc / NZ)
        phase[index, 0] = jnp.cos(theta) * keep
        phase[index, 1] = jnp.sin(theta) * keep

    for h in range(2):
        q = q_rows(h)

        def tile_phase(n, carry):
            write_phase(h * HALF + n, q, (own * TILES + h * HALF + n) * LANES, 1.0)
            return carry

        lax.fori_loop(0, HALF, tile_phase, 0)
        if h == 0:
            keep = (own < 6).astype(jnp.float32)
            write_phase(TILES, q, (ROW * TILES + own % 2) * LANES, keep)

    acc[...] = jnp.zeros_like(acc)

    def wait_tile(t, group):
        block = buf.at[pl.ds(t * SLOTS + 4 * group, 4)]
        pltpu.make_async_copy(block, block, recv_sem.at[t, group]).wait()

    def wait_extra(group):
        block = xbuf.at[pl.ds(4 * group, 4)]
        pltpu.make_async_copy(block, block, xrecv_sem.at[group]).wait()

    def forward(src, dst, ssem, rsem, target):
        return pltpu.make_async_remote_copy(
            src_ref=src, dst_ref=dst, send_sem=ssem, recv_sem=rsem,
            device_id=at(target, own), device_id_type=MESH,
        )

    def forward_extra():
        return forward(xbuf.at[pl.ds(0, 4)], xbuf.at[pl.ds(8, 4)], xfsend_sem, xrecv_sem.at[2], row_down)

    def forward_low(t):
        return forward(
            buf.at[pl.ds(t * SLOTS, 4)], buf.at[pl.ds(t * SLOTS + 8, 4)],
            fsend_sem.at[t], recv_sem.at[t, 2], row_down,
        )

    def forward_high(t):
        return forward(
            buf.at[pl.ds(t * SLOTS + 8, 4)], buf.at[pl.ds(t * SLOTS, 4)],
            fsend_sem.at[t], recv_sem.at[t, 0], row_up,
        )

    wait_extra(0)
    forward_extra().start()

    def forward_tiles(n, carry):
        wait_tile(n, 0)
        forward_low(n).start()
        wait_tile(n + HALF, 2)
        forward_high(n + HALF).start()
        return carry

    lax.fori_loop(0, HALF, forward_tiles, 0)

    def pair_products(left, rights):
        left_high, left_low = split(left)
        right_high, right_low = split(jnp.concatenate(rights, axis=0))
        return (
            contract(left_high, right_high)
            + contract(left_high, right_low)
            + contract(left_low, right_high)
        )

    def rotate(real, imag, index, d, i, comps):
        c = phase[index, 0, pl.ds(d * 8 + i, 1), :]
        s = phase[index, 1, pl.ds(d * 8 + i, 1), :]
        c = jnp.concatenate([jnp.broadcast_to(c, (32, LANES))] * comps, axis=1)
        s = jnp.concatenate([jnp.broadcast_to(s, (32, LANES))] * comps, axis=1)
        return [c * real - s * imag, s * real + c * imag]

    def extra_step(i, carry):
        left = xbuf[i].reshape(64, LANES)
        rights = []
        for d, offset in enumerate((1, 4)):
            rights += rotate(xbuf[i + offset, 0], xbuf[i + offset, 1], TILES, d, i, 1)
        acc[i + 4] += pair_products(left, rights)
        return carry

    def wide(slot, part):
        return jnp.concatenate([buf[slot, part, comp] for comp in range(3)], axis=1)

    def tile_step(t, shift, i):
        base = t * SLOTS + i
        left = jnp.concatenate([wide(base, 0), wide(base, 1)], axis=0)
        rights = []
        for d, offset in enumerate((1, 4)):
            rights += rotate(wide(base + offset, 0), wide(base + offset, 1), t, d, i, 3)
        acc[i + shift] += pair_products(left, rights)

    wait_extra(1)
    wait_extra(2)
    lax.fori_loop(0, 8, extra_step, 0)

    def tiles(n, carry):
        wait_tile(n + HALF, 0)
        wait_tile(n + HALF, 1)

        def high_step(i, c):
            tile_step(n + HALF, 0, i)
            return c

        lax.fori_loop(0, 8, high_step, 0)
        wait_tile(n, 1)
        wait_tile(n, 2)

        def low_step(i, c):
            tile_step(n, 4, i)
            return c

        lax.fori_loop(0, 8, low_step, 0)
        return carry

    lax.fori_loop(0, HALF, tiles, 0)

    pl.semaphore_wait(rows_sem, 2)
    lane32 = lax.broadcasted_iota(jnp.int32, (32, LANES), 1)
    lane16 = lax.broadcasted_iota(jnp.int32, (16, LANES), 1)

    def reduce_copies(a, holder):
        k = (row * ROW + a - 4 + 32) % 32
        slot = holder * ROW + own
        return [
            (stage.at[a], reduced.at[slot, pl.ds(0, 2)], 0, k),
            (stage.at[a, pl.ds(0, 1)], reduced.at[slot, pl.ds(2, 1)], 1, (k + 1) % 32),
            (stage.at[a, pl.ds(1, 1)], reduced.at[slot, pl.ds(3, 1)], 2, (k + 4) % 32),
        ]

    for a in range(SLOTS):
        top = acc[a, pl.ds(0, 32), :]
        bottom = acc[a, pl.ds(32, 32), :]
        swapped = jnp.where(
            lane32 % 64 < 32, pltpu.roll(bottom, 96, 1), -pltpu.roll(bottom, 32, 1)
        )
        value = top + swapped
        turned = pltpu.roll(value, 64, 1)
        stage[a, 0] = jnp.where(lane16 < 64, value[:16], turned[16:])
        stage[a, 1] = jnp.where(lane16 < 64, turned[:16], value[16:])
        for src, dst, kind, target in reduce_copies(a, 1 if a < 4 else 0):
            @pl.when(target == me)
            def _():
                pltpu.make_async_copy(src, dst, rrecv_sem.at[kind, 1 if a < 4 else 0]).start()

            @pl.when(target != me)
            def _():
                pltpu.make_async_remote_copy(
                    src_ref=src, dst_ref=dst, send_sem=rsend_sem.at[a, kind],
                    recv_sem=rrecv_sem.at[kind, 1 if a < 4 else 0],
                    device_id={"ka": target}, device_id_type=MESH,
                ).start()

    def wait_reduced(kind, holder):
        first, count = ((0, 2), (2, 1), (3, 1))[kind]
        block = reduced.at[pl.ds(holder * ROW, ROW), pl.ds(first, count)]
        pltpu.make_async_copy(block, block, rrecv_sem.at[kind, holder]).wait()

    def sum_reduced(kind, holder):
        first, count = ((0, 2), (2, 1), (3, 1))[kind]
        value = reduced[holder * ROW, pl.ds(first, count)]
        for j in range(1, ROW):
            value = value + reduced[holder * ROW + j, pl.ds(first, count)]
        return value

    for kind in range(3):
        first, count = ((0, 2), (2, 1), (3, 1))[kind]
        wait_reduced(kind, 0)
        total[pl.ds(first, count)] = sum_reduced(kind, 0)
        source = (own - (0, 1, 4)[kind] + ROW) % ROW

        @pl.when(source >= 4)
        def _():
            wait_reduced(kind, 1)
            total[pl.ds(first, count)] += sum_reduced(kind, 1)

    def slab_copy(dx):
        return pltpu.make_async_remote_copy(
            src_ref=total, dst_ref=gathered.at[gx], send_sem=gsend_sem.at[dx - 1], recv_sem=grecv_sem,
            device_id={"gz": (gx + dx) % 4}, device_id_type=MESH,
        )

    for dx in (1, 2, 3):
        slab_copy(dx).start()
    gathered[gx] = total[...]
    block = gathered.at[pl.ds(0, 3)]
    pltpu.make_async_copy(block, block, grecv_sem).wait()
    summed = gathered[0] + gathered[1] + gathered[2] + gathered[3]
    for index, direction in ((0, 0), (1, 2), (2, 1), (3, 3)):
        value = summed[index]
        real = jnp.concatenate([value[:, 0:32], value[:, 64:96]], axis=0)
        imag = jnp.concatenate([value[:, 32:64], value[:, 96:128]], axis=0)
        if index < 2:
            out_ref[direction, 0] = real
            out_ref[direction, 1] = imag
        else:
            out_ref[direction, 0] = real.T
            out_ref[direction, 1] = -imag.T

    for p in peers:
        pass
    seven = xbuf.at[pl.ds(0, 7)]
    pltpu.make_async_copy(seven, seven, xsend_sem).wait()
    forward_extra().wait_send()

    def drain(t, carry):
        block = buf.at[pl.ds(t * SLOTS, 7)]
        pltpu.make_async_copy(block, block, send_sem.at[t]).wait()
        block = buf.at[pl.ds(t * SLOTS, 4)]
        pltpu.make_async_copy(block, block, fsend_sem.at[t]).wait()
        return carry

    lax.fori_loop(0, TILES, drain, 0)
    for a in range(SLOTS):
        for src, dst, kind, target in reduce_copies(a, 1 if a < 4 else 0):
            @pl.when(target != me)
            def _():
                pltpu.make_async_copy(src, src, rsend_sem.at[a, kind]).wait()
    for dx in (1, 2, 3):
        slab_copy(dx).wait_send()


def per_device(fields, bvectors, gshift):
    local = jnp.transpose(fields[0], (0, 2, 1, 3))
    dma = pltpu.SemaphoreType.DMA
    f32 = jnp.float32
    result = pl.pallas_call(
        kernel,
        out_shape=jax.ShapeDtypeStruct((4, 2, 32, 32), f32),
        in_specs=[
            pl.BlockSpec(memory_space=pltpu.SMEM),
            pl.BlockSpec(memory_space=pltpu.SMEM),
            pl.BlockSpec(memory_space=pltpu.HBM),
        ],
        out_specs=pl.BlockSpec(memory_space=pltpu.VMEM),
        scratch_shapes=[
            pltpu.VMEM((TILES * SLOTS, 2, 3, 32, LANES), f32),
            pltpu.VMEM((SLOTS, 2, 32, LANES), f32),
            pltpu.VMEM((TILES + 1, 2, 16, LANES), f32),
            pltpu.VMEM((SLOTS, 64, LANES), f32),
            pltpu.VMEM((SLOTS, 2, 16, LANES), f32),
            pltpu.VMEM((2 * ROW, 4, 16, LANES), f32),
            pltpu.VMEM((4, 16, LANES), f32),
            pltpu.VMEM((4, 4, 16, LANES), f32),
            dma((TILES,)),
            dma((TILES, 3)),
            dma,
            dma((3,)),
            dma((TILES,)),
            dma,
            dma((SLOTS, 3)),
            dma((3, 2)),
            dma((3,)),
            dma,
            pltpu.SemaphoreType.REGULAR,
        ],
        compiler_params=pltpu.CompilerParams(
            collective_id=0, has_side_effects=True, vmem_limit_bytes=40 * 1024 * 1024
        ),
        name="wannier",
    )(bvectors, jnp.transpose(gshift, (2, 1, 0)), local)
    return result[None]


def solution(mesh):
    in_specs = (P("ka", None, None, None, "gz"), P(), P())
    out_specs = P("ka", None, None, None, None)
    return jax.shard_map(
        per_device, mesh=mesh, in_specs=in_specs, out_specs=out_specs, check_vma=False
    )
```

profile of v0, /device:TPU:1, one launch (start us, length us, event | category | flops | bytes accessed | tf_op | source)
XLA Modules:
  0.0 82.6 jit_solution(15326975565407448173)
XLA Ops:
  0.0 0.0 copy-start
  0.0 2.4 %copy-done = f32[1,2,32,3,6400]{4,2,3,1,0:T(8,128)S(1)} copy-done((f32[1,2,32,3,6400]{4,2,3,1,0:T(8,128)S(1)}, f32[1,2,32,3,6400]{4,2,3,1,0:T(8,128)}, u32[]{:S(2)}) %copy-start) | copy-done | bytes 4915224
  2.4 0.0 copy-start.1
  2.4 0.7 copy-done.1
  3.1 0.0 copy-start.2
  3.1 0.7 copy-done.2
  3.8 78.2 %wannier.1 = f32[4,2,32,32]{3,2,1,0:T(8,128)S(1)} custom-call(f32[2,3]{1,0:T(2,128)S(1)} %copy-done.2, s32[3,2,32]{2,1,0:T(2,128)S(1)} %bitcast.7, f32[2,3,32,6400]{3,2,1,0:T(8,128)S(1)} %bitcast.5), custom_call_target="tpu_custom_call" | custom-call | tf_op jit(solution)/shard_map/wannier/pallas_call | solution.py:353
  82.0 0.7 copy.5
Async XLA Ops:
  0.0 2.4 %copy-start = (f32[1,2,32,3,6400]{4,2,3,1,0:T(8,128)S(1)}, f32[1,2,32,3,6400]{4,2,3,1,0:T(8,128)}, u32[]{:S(2)}) copy-start(f32[1,2,32,3,6400]{4,2,3,1,0:T(8,128)} %param.3) | copy-start | bytes 14745604
  2.4 0.7 copy-start.1
  3.1 0.7 copy-start.2
where the time goes:
time: 83.1 us; the launch traced here: 82.6 us
  Pallas kernels  78.2 us (94%)
  local copies, waits for them, and re-layouts  4.41 us (5%)
    pallas_call x1, Pallas kernels, per_device(): pl.pallas_call(kernel, out_shape=jax.ShapeDtypeStruct((4, 2, 32, 32), f32...  78.2 us
    unnamed x7, local copies, waits for them, and re-layouts  4.41 us

commit v1 on v0

v1 whole, which is shorter than its diff:
```python
import math

import jax
import jax.numpy as jnp
from jax import lax
from jax.experimental import pallas as pl
from jax.experimental.pallas import tpu as pltpu
from jax.sharding import PartitionSpec as P

GX = 40
GY = 40
NZ = 16
ROW = 8
ROWS = 4
SLOTS = 12
TILES = 6
LANES = 128
MESH = pl.DeviceIdType.MESH
TWO_PI = 2.0 * math.pi


def split(value):
    high = value.astype(jnp.bfloat16)
    low = (value - high.astype(jnp.float32)).astype(jnp.bfloat16)
    return high, low


def contract(left, right):
    return lax.dot_general(
        left, right, (((1,), (1,)), ((), ())), preferred_element_type=jnp.float32
    )


def kernel(
    bvec_hbm, gshift_hbm, field_ref, out_ref,
    bvec_ref, gshift_ref, buf, xbuf, phase, acc, stage, reduced, total, gathered,
    small_sem, send_sem, recv_sem, xsend_sem, xrecv_sem, fsend_sem, xfsend_sem,
    rsend_sem, rrecv_sem, gsend_sem, grecv_sem, rows_sem,
):
    me = lax.axis_index("ka")
    gx = lax.axis_index("gz")
    row = me // ROW
    own = me % ROW
    zpos = own // 2
    core = own % 2
    side = zpos // 2
    row_up = (row + 1) % ROWS
    row_down = (row + ROWS - 1) % ROWS
    pass_row = jnp.where(core == 0, row_down, row_up)
    pass_from = 8 * core
    pass_to = 8 - 8 * core
    first_k = row * ROW - 4 * core

    def at(r, j):
        return {"ka": r * ROW + j}

    small = [
        pltpu.make_async_copy(bvec_hbm, bvec_ref, small_sem.at[0]),
        pltpu.make_async_copy(gshift_hbm, gshift_ref, small_sem.at[1]),
    ]
    for copy in small:
        copy.start()

    sibling = zpos * 2 + 1 - core
    others = [((zpos + dz) % 4) * 2 for dz in (2, 1, 3)]
    peers = [z + c for z in others for c in range(2)] + [sibling]

    barrier = pltpu.get_barrier_semaphore()
    for p in peers:
        pl.semaphore_signal(barrier, inc=1, device_id=at(row, p), device_id_type=MESH)
    for r in (row_up, row_down):
        pl.semaphore_signal(barrier, inc=1, device_id=at(r, own), device_id_type=MESH)
    for dx in (1, 2, 3):
        pl.semaphore_signal(barrier, inc=1, device_id={"gz": (gx + dx) % 4}, device_id_type=MESH)
    pl.semaphore_wait(barrier, 12)

    def extra_source(p):
        comp = jnp.minimum(p // 2, 2)
        start = pl.multiple_of((ROW * TILES + p % 2) * LANES, LANES)
        return field_ref.at[:, comp, :, pl.ds(start, LANES)]

    def tile_source(p, t):
        start = pl.multiple_of((p * TILES + t) * LANES, LANES)
        return field_ref.at[:, :, :, pl.ds(start, LANES)]

    def send_extra(p, c):
        return pltpu.make_async_remote_copy(
            src_ref=extra_source(p), dst_ref=xbuf.at[own + 4 * c],
            send_sem=xsend_sem, recv_sem=xrecv_sem.at[side + c],
            device_id=at(row, p), device_id_type=MESH,
        )

    def send_tile(p, c, t):
        return pltpu.make_async_remote_copy(
            src_ref=tile_source(p, t), dst_ref=buf.at[t * SLOTS + own + 4 * c],
            send_sem=send_sem.at[t], recv_sem=recv_sem.at[t, side + c],
            device_id=at(row, p), device_id_type=MESH,
        )

    for z in others:
        for c in range(2):
            send_extra(z + c, c).start()
    send_extra(sibling, 1 - core).start()
    pltpu.make_async_copy(
        extra_source(own), xbuf.at[own + 4 * core], xrecv_sem.at[side + core]
    ).start()

    def send_first(t, carry):
        for z in others:
            send_tile(z + side, side, t).start()
        send_tile(sibling, 1 - core, t).start()
        pltpu.make_async_copy(
            tile_source(own, t), buf.at[t * SLOTS + own + 4 * core], recv_sem.at[t, side + core]
        ).start()
        return carry

    def send_second(t, carry):
        for z in others:
            send_tile(z + 1 - side, 1 - side, t).start()
        return carry

    lax.fori_loop(0, TILES, send_first, 0)
    lax.fori_loop(0, TILES, send_second, 0)

    for r in (row_up, row_down):
        pl.semaphore_signal(rows_sem, inc=1, device_id=at(r, own), device_id_type=MESH)

    for copy in small:
        copy.wait()

    row_id = lax.broadcasted_iota(jnp.int32, (16, LANES), 0)
    lane = lax.broadcasted_iota(jnp.int32, (16, LANES), 1).astype(jnp.float32)
    q = []
    for a in range(3):
        values = jnp.zeros((16, LANES), jnp.float32)
        for d in range(2):
            for i in range(8):
                k = (first_k + i + 32) % 32
                value = bvec_ref[d, a] + gshift_ref[a, d, k].astype(jnp.float32)
                values = jnp.where(row_id == d * 8 + i, value, values)
        q.append(values)

    def write_phase(index, start, keep):
        cell = lane + start.astype(jnp.float32)
        line = jnp.floor((cell + 0.5) * (1.0 / GX))
        plane = jnp.floor((cell + 0.5) * (1.0 / (GX * GY)))
        xc = cell - GX * line
        yc = line - GY * plane
        zc = plane + (gx * 4).astype(jnp.float32)
        theta = -TWO_PI * (q[0] * xc / GX + q[1] * yc / GY + q[2] * zc / NZ)
        phase[index, 0] = jnp.cos(theta) * keep
        phase[index, 1] = jnp.sin(theta) * keep

    def tile_phase(t, carry):
        write_phase(t, (own * TILES + t) * LANES, 1.0)
        return carry

    lax.fori_loop(0, TILES, tile_phase, 0)
    write_phase(TILES, (ROW * TILES + own % 2) * LANES, (own < 6).astype(jnp.float32))
    acc[...] = jnp.zeros_like(acc)

    def wait_tile(t, group):
        block = buf.at[pl.ds(t * SLOTS + 4 * group, 4)]
        pltpu.make_async_copy(block, block, recv_sem.at[t, group]).wait()

    def wait_extra(group):
        block = xbuf.at[pl.ds(4 * group, 4)]
        pltpu.make_async_copy(block, block, xrecv_sem.at[group]).wait()

    pass_extra = pltpu.make_async_remote_copy(
        src_ref=xbuf.at[pl.ds(pass_from, 4)], dst_ref=xbuf.at[pl.ds(pass_to, 4)],
        send_sem=xfsend_sem, recv_sem=xrecv_sem.at[2 - 2 * core],
        device_id=at(pass_row, own), device_id_type=MESH,
    )

    def pass_tile(t, carry):
        wait_tile(t, 2 * core)
        pltpu.make_async_remote_copy(
            src_ref=buf.at[pl.ds(t * SLOTS + pass_from, 4)],
            dst_ref=buf.at[pl.ds(t * SLOTS + pass_to, 4)],
            send_sem=fsend_sem.at[t], recv_sem=recv_sem.at[t, 2 - 2 * core],
            device_id=at(pass_row, own), device_id_type=MESH,
        ).start()
        return carry

    wait_extra(2 * core)
    pass_extra.start()
    lax.fori_loop(0, TILES, pass_tile, 0)

    def pair_products(left, rights):
        left_high, left_low = split(left)
        right_high, right_low = split(jnp.concatenate(rights, axis=0))
        return (
            contract(left_high, right_high)
            + contract(left_high, right_low)
            + contract(left_low, right_high)
        )

    def rotate(real, imag, index, d, i, comps):
        c = phase[index, 0, pl.ds(d * 8 + i, 1), :]
        s = phase[index, 1, pl.ds(d * 8 + i, 1), :]
        c = jnp.concatenate([jnp.broadcast_to(c, (32, LANES))] * comps, axis=1)
        s = jnp.concatenate([jnp.broadcast_to(s, (32, LANES))] * comps, axis=1)
        return [c * real - s * imag, s * real + c * imag]

    def extra_step(i):
        left = xbuf[i].reshape(64, LANES)
        rights = []
        for d, offset in enumerate((1, 4)):
            rights += rotate(xbuf[i + offset, 0], xbuf[i + offset, 1], TILES, d, i, 1)
        acc[i] += pair_products(left, rights)

    def wide(slot, part):
        return jnp.concatenate([buf[slot, part, comp] for comp in range(3)], axis=1)

    def tile_step(t, i):
        base = t * SLOTS + i
        left = jnp.concatenate([wide(base, 0), wide(base, 1)], axis=0)
        rights = []
        for d, offset in enumerate((1, 4)):
            rights += rotate(wide(base + offset, 0), wide(base + offset, 1), t, d, i, 3)
        acc[i] += pair_products(left, rights)

    lane32 = lax.broadcasted_iota(jnp.int32, (32, LANES), 1)
    lane16 = lax.broadcasted_iota(jnp.int32, (16, LANES), 1)
    holder = core * 4 + zpos
    kinds = ((0, 2), (2, 1), (3, 1))

    def reduce_copies(i):
        k = first_k + i + 32
        return [
            (stage.at[i], reduced.at[holder, pl.ds(0, 2)], 0, k % 32),
            (stage.at[i, pl.ds(0, 1)], reduced.at[holder, pl.ds(2, 1)], 1, (k + 1) % 32),
            (stage.at[i, pl.ds(1, 1)], reduced.at[holder, pl.ds(3, 1)], 2, (k + 4) % 32),
        ]

    def send_matrices(i):
        top = acc[i, pl.ds(0, 32), :]
        bottom = acc[i, pl.ds(32, 32), :]
        swapped = jnp.where(
            lane32 % 64 < 32, pltpu.roll(bottom, 96, 1), -pltpu.roll(bottom, 32, 1)
        )
        value = top + swapped
        turned = pltpu.roll(value, 64, 1)
        stage[i, 0] = jnp.where(lane16 < 64, value[:16], turned[16:])
        stage[i, 1] = jnp.where(lane16 < 64, turned[:16], value[16:])
        for src, dst, kind, target in reduce_copies(i):
            @pl.when(target == me)
            def _():
                pltpu.make_async_copy(src, dst, rrecv_sem.at[kind]).start()

            @pl.when(target != me)
            def _():
                pltpu.make_async_remote_copy(
                    src_ref=src, dst_ref=dst, send_sem=rsend_sem.at[i, kind],
                    recv_sem=rrecv_sem.at[kind],
                    device_id={"ka": target}, device_id_type=MESH,
                ).start()

    def loop(step):
        def body(m, carry):
            step(2 * m)
            step(2 * m + 1)
            return carry

        lax.fori_loop(0, 4, body, 0)

    wait_extra(1)
    wait_extra(2 - 2 * core)
    loop(extra_step)

    def tiles(t, carry):
        wait_tile(t, 2 - 2 * core)
        wait_tile(t, 1)
        loop(lambda i: tile_step(t, i))
        return carry

    lax.fori_loop(0, TILES - 1, tiles, 0)
    pl.semaphore_wait(rows_sem, 2)
    wait_tile(TILES - 1, 2 - 2 * core)
    wait_tile(TILES - 1, 1)

    def last(m, carry):
        tile_step(TILES - 1, 2 * m)
        tile_step(TILES - 1, 2 * m + 1)
        send_matrices(2 * m)
        send_matrices(2 * m + 1)
        return carry

    lax.fori_loop(0, 4, last, 0)

    for kind, (first, count) in enumerate(kinds):
        block = reduced.at[:, pl.ds(first, count)]
        pltpu.make_async_copy(block, block, rrecv_sem.at[kind]).wait()
        value = reduced[0, pl.ds(first, count)]
        for j in range(1, ROW):
            value = value + reduced[j, pl.ds(first, count)]
        total[pl.ds(first, count)] = value

    def slab_copy(dx):
        return pltpu.make_async_remote_copy(
            src_ref=total, dst_ref=gathered.at[gx], send_sem=gsend_sem.at[dx - 1], recv_sem=grecv_sem,
            device_id={"gz": (gx + dx) % 4}, device_id_type=MESH,
        )

    for dx in (2, 1, 3):
        slab_copy(dx).start()
    gathered[gx] = total[...]

    seven = xbuf.at[pl.ds(0, 7)]
    pltpu.make_async_copy(seven, seven, xsend_sem).wait()
    pass_extra.wait_send()

    def drain(t, carry):
        block = buf.at[pl.ds(t * SLOTS, 7)]
        pltpu.make_async_copy(block, block, send_sem.at[t]).wait()
        block = buf.at[pl.ds(t * SLOTS, 4)]
        pltpu.make_async_copy(block, block, fsend_sem.at[t]).wait()
        return carry

    lax.fori_loop(0, TILES, drain, 0)

    def drain_matrices(i, carry):
        for src, dst, kind, target in reduce_copies(i):
            @pl.when(target != me)
            def _():
                pltpu.make_async_copy(src, src, rsend_sem.at[i, kind]).wait()
        return carry

    lax.fori_loop(0, 8, drain_matrices, 0)

    block = gathered.at[pl.ds(0, 3)]
    pltpu.make_async_copy(block, block, grecv_sem).wait()
    summed = gathered[0] + gathered[1] + gathered[2] + gathered[3]
    for index, direction in ((0, 0), (1, 2), (2, 1), (3, 3)):
        value = summed[index]
        real = jnp.concatenate([value[:, 0:32], value[:, 64:96]], axis=0)
        imag = jnp.concatenate([value[:, 32:64], value[:, 96:128]], axis=0)
        if index < 2:
            out_ref[direction, 0] = real
            out_ref[direction, 1] = imag
        else:
            out_ref[direction, 0] = real.T
            out_ref[direction, 1] = -imag.T
    for dx in (1, 2, 3):
        slab_copy(dx).wait_send()


def per_device(fields, bvectors, gshift):
    local = jnp.transpose(fields[0], (0, 2, 1, 3))
    dma = pltpu.SemaphoreType.DMA
    f32 = jnp.float32
    result = pl.pallas_call(
        kernel,
        out_shape=jax.ShapeDtypeStruct((4, 2, 32, 32), f32),
        in_specs=[
            pl.BlockSpec(memory_space=pltpu.HBM),
            pl.BlockSpec(memory_space=pltpu.HBM),
            pl.BlockSpec(memory_space=pltpu.HBM),
        ],
        out_specs=pl.BlockSpec(memory_space=pltpu.VMEM),
        scratch_shapes=[
            pltpu.SMEM((2, 3), f32),
            pltpu.SMEM((3, 2, 32), jnp.int32),
            pltpu.VMEM((TILES * SLOTS, 2, 3, 32, LANES), f32),
            pltpu.VMEM((SLOTS, 2, 32, LANES), f32),
            pltpu.VMEM((TILES + 1, 2, 16, LANES), f32),
            pltpu.VMEM((ROW, 64, LANES), f32),
            pltpu.VMEM((ROW, 2, 16, LANES), f32),
            pltpu.VMEM((ROW, 4, 16, LANES), f32),
            pltpu.VMEM((4, 16, LANES), f32),
            pltpu.VMEM((4, 4, 16, LANES), f32),
            dma((2,)),
            dma((TILES,)),
            dma((TILES, 3)),
            dma,
            dma((3,)),
            dma((TILES,)),
            dma,
            dma((ROW, 3)),
            dma((3,)),
            dma((3,)),
            dma,
            pltpu.SemaphoreType.REGULAR,
        ],
        compiler_params=pltpu.CompilerParams(
            collective_id=0, has_side_effects=True, vmem_limit_bytes=60 * 1024 * 1024
        ),
        name="wannier",
    )(bvectors, jnp.transpose(gshift, (2, 1, 0)), local)
    return result[None]


def solution(mesh):
    in_specs = (P("ka", None, None, None, "gz"), P(), P())
    out_specs = P("ka", None, None, None, None)
    return jax.shard_map(
        per_device, mesh=mesh, in_specs=in_specs, out_specs=out_specs, check_vma=False
    )
```

time: 83.1 us -> 75.7 us (0.911)
  Pallas kernels: 78.2 us -> 73.4 us
  local copies, waits for them, and re-layouts: 4.41 us -> 1.57 us
    pallas_call x1, Pallas kernels: 78.2 us -> 73.4 us  [per_device(): pl.pallas_call(kernel, out_shape=jax.ShapeDtypeStruct((4, 2, 32, 32), f32...]
    unnamed x7 -> x1, local copies, waits for them, and re-layouts: 4.41 us -> 1.57 us
where the time goes in v1:
time: 75.7 us; the launch traced here: 74.9 us
  Pallas kernels  73.4 us (97%)
  local copies, waits for them, and re-layouts  1.57 us (2%)
    pallas_call x1, Pallas kernels, per_device(): pl.pallas_call(kernel, out_shape=jax.ShapeDtypeStruct((4, 2, 32, 32), f32...  73.4 us
    unnamed x1, local copies, waits for them, and re-layouts  1.57 us

profile of v1, /device:TPU:1, one launch (start us, length us, event | category | flops | bytes accessed | tf_op | source)
XLA Modules:
  0.0 74.9 jit_solution(13017002528650439704)
XLA Ops:
  0.0 73.4 %wannier.1 = f32[4,2,32,32]{3,2,1,0:T(8,128)} custom-call(f32[2,3]{1,0:T(2,128)} %bvec_hbm.1, s32[3,2,32]{2,1,0:T(2,128)} %bitcast.7, f32[2,3,32,6400]{3,2,1,0:T(8,128)} %bitcast.5), custom_call_target="tpu_custom_call" | custom-call | tf_op jit(solution)/shard_map/wannier/pallas_call | solution.py:353
  73.4 1.6 %copy.5 = f32[1,4,2,32,32]{4,3,2,1,0:T(8,128)} copy(f32[1,4,2,32,32]{4,3,2,1,0:T(8,128)} %bitcast.6) | data formatting | bytes 65536

commit v2 on v1

--- a/solution.py
+++ b/solution.py
@@ -15,6 +15,7 @@
 SLOTS = 12
 TILES = 6
 LANES = 128
+UNROLL = 8
 MESH = pl.DeviceIdType.MESH
 TWO_PI = 2.0 * math.pi
 
@@ -98,8 +99,7 @@
         )
 
     for z in others:
-        for c in range(2):
-            send_extra(z + c, c).start()
+        send_extra(z + side, side).start()
     send_extra(sibling, 1 - core).start()
     pltpu.make_async_copy(
         extra_source(own), xbuf.at[own + 4 * core], xrecv_sem.at[side + core]
@@ -121,6 +121,8 @@
 
     lax.fori_loop(0, TILES, send_first, 0)
     lax.fori_loop(0, TILES, send_second, 0)
+    for z in others:
+        send_extra(z + 1 - side, 1 - side).start()
 
     for r in (row_up, row_down):
         pl.semaphore_signal(rows_sem, inc=1, device_id=at(r, own), device_id_type=MESH)
@@ -224,17 +226,30 @@
     lane32 = lax.broadcasted_iota(jnp.int32, (32, LANES), 1)
     lane16 = lax.broadcasted_iota(jnp.int32, (16, LANES), 1)
     holder = core * 4 + zpos
-    kinds = ((0, 2), (2, 1), (3, 1))
-
-    def reduce_copies(i):
-        k = first_k + i + 32
-        return [
-            (stage.at[i], reduced.at[holder, pl.ds(0, 2)], 0, k % 32),
-            (stage.at[i, pl.ds(0, 1)], reduced.at[holder, pl.ds(2, 1)], 1, (k + 1) % 32),
-            (stage.at[i, pl.ds(1, 1)], reduced.at[holder, pl.ds(3, 1)], 2, (k + 4) % 32),
-        ]
-
-    def send_matrices(i):
+    spans = [(0, 2)] + [(0, 3)] * 3 + [(0, 4)] * 4 + [(2, 2)] + [(3, 1)] * 3
+
+    def target_copy(i):
+        part = pl.ds(*spans[i])
+        target = (first_k + i + 32) % 32
+        return target, pltpu.make_async_remote_copy(
+            src_ref=stage.at[i, part], dst_ref=reduced.at[holder, part],
+            send_sem=rsend_sem.at[i], recv_sem=rrecv_sem,
+            device_id={"ka": target}, device_id_type=MESH,
+        )
+
+    def send_target(i):
+        part = pl.ds(*spans[i])
+        target, copy = target_copy(i)
+
+        @pl.when(target == me)
+        def _():
+            pltpu.make_async_copy(stage.at[i, part], reduced.at[holder, part], rrecv_sem).start()
+
+        @pl.when(target != me)
+        def _():
+            copy.start()
+
+    def finish_matrices(i):
         top = acc[i, pl.ds(0, 32), :]
         bottom = acc[i, pl.ds(32, 32), :]
         swapped = jnp.where(
@@ -242,70 +257,50 @@
         )
         value = top + swapped
         turned = pltpu.roll(value, 64, 1)
-        stage[i, 0] = jnp.where(lane16 < 64, value[:16], turned[16:])
-        stage[i, 1] = jnp.where(lane16 < 64, turned[:16], value[16:])
-        for src, dst, kind, target in reduce_copies(i):
-            @pl.when(target == me)
-            def _():
-                pltpu.make_async_copy(src, dst, rrecv_sem.at[kind]).start()
-
-            @pl.when(target != me)
-            def _():
-                pltpu.make_async_remote_copy(
-                    src_ref=src, dst_ref=dst, send_sem=rsend_sem.at[i, kind],
-                    recv_sem=rrecv_sem.at[kind],
-                    device_id={"ka": target}, device_id_type=MESH,
-                ).start()
-
-    def loop(step):
-        def body(m, carry):
-            step(2 * m)
-            step(2 * m + 1)
-            return carry
-
-        lax.fori_loop(0, 4, body, 0)
-
-    wait_extra(1)
-    wait_extra(2 - 2 * core)
-    loop(extra_step)
+        along_x = jnp.where(lane16 < 64, value[:16], turned[16:])
+        along_y = jnp.where(lane16 < 64, turned[:16], value[16:])
+        stage[i, 0] = along_x
+        stage[i, 1] = along_y
+        stage[i + 1, 2] = along_x
+        stage[i + 4, 3] = along_y
 
     def tiles(t, carry):
         wait_tile(t, 2 - 2 * core)
         wait_tile(t, 1)
-        loop(lambda i: tile_step(t, i))
-        return carry
-
-    lax.fori_loop(0, TILES - 1, tiles, 0)
+
+        def body(m, inner):
+            for u in range(UNROLL):
+                tile_step(t, UNROLL * m + u)
+            return inner
+
+        lax.fori_loop(0, ROW // UNROLL, body, 0)
+        return carry
+
+    lax.fori_loop(0, TILES, tiles, 0)
     pl.semaphore_wait(rows_sem, 2)
-    wait_tile(TILES - 1, 2 - 2 * core)
-    wait_tile(TILES - 1, 1)
-
-    def last(m, carry):
-        tile_step(TILES - 1, 2 * m)
-        tile_step(TILES - 1, 2 * m + 1)
-        send_matrices(2 * m)
-        send_matrices(2 * m + 1)
-        return carry
-
-    lax.fori_loop(0, 4, last, 0)
-
-    for kind, (first, count) in enumerate(kinds):
-        block = reduced.at[:, pl.ds(first, count)]
-        pltpu.make_async_copy(block, block, rrecv_sem.at[kind]).wait()
-        value = reduced[0, pl.ds(first, count)]
-        for j in range(1, ROW):
-            value = value + reduced[j, pl.ds(first, count)]
-        total[pl.ds(first, count)] = value
+    wait_extra(2 - 2 * core)
+    wait_extra(1)
+    for i in range(ROW):
+        extra_step(i)
+        finish_matrices(i)
+    for i in range(SLOTS):
+        send_target(i)
 
     def slab_copy(dx):
         return pltpu.make_async_remote_copy(
-            src_ref=total, dst_ref=gathered.at[gx], send_sem=gsend_sem.at[dx - 1], recv_sem=grecv_sem,
+            src_ref=total, dst_ref=gathered.at[gx],
+            send_sem=gsend_sem.at[dx - 1], recv_sem=grecv_sem,
             device_id={"gz": (gx + dx) % 4}, device_id_type=MESH,
         )
 
+    pltpu.make_async_copy(reduced, reduced, rrecv_sem).wait()
+    value = reduced[0]
+    for j in range(1, ROW):
+        value = value + reduced[j]
+    total[...] = value
     for dx in (2, 1, 3):
         slab_copy(dx).start()
-    gathered[gx] = total[...]
+    gathered[gx] = value
 
     seven = xbuf.at[pl.ds(0, 7)]
     pltpu.make_async_copy(seven, seven, xsend_sem).wait()
@@ -320,14 +315,12 @@
 
     lax.fori_loop(0, TILES, drain, 0)
 
-    def drain_matrices(i, carry):
-        for src, dst, kind, target in reduce_copies(i):
-            @pl.when(target != me)
-            def _():
-                pltpu.make_async_copy(src, src, rsend_sem.at[i, kind]).wait()
-        return carry
-
-    lax.fori_loop(0, 8, drain_matrices, 0)
+    for i in range(SLOTS):
+        target, copy = target_copy(i)
+
+        @pl.when(target != me)
+        def _():
+            copy.wait_send()
 
     block = gathered.at[pl.ds(0, 3)]
     pltpu.make_async_copy(block, block, grecv_sem).wait()
@@ -347,7 +340,12 @@
 
 
 def per_device(fields, bvectors, gshift):
-    local = jnp.transpose(fields[0], (0, 2, 1, 3))
+    local, vectors, shifts = (
+        pltpu.with_memory_space_constraint(value, pltpu.HBM)
+        for value in (
+            jnp.transpose(fields[0], (0, 2, 1, 3)), bvectors, jnp.transpose(gshift, (2, 1, 0))
+        )
+    )
     dma = pltpu.SemaphoreType.DMA
     f32 = jnp.float32
     result = pl.pallas_call(
@@ -366,7 +364,7 @@
             pltpu.VMEM((SLOTS, 2, 32, LANES), f32),
             pltpu.VMEM((TILES + 1, 2, 16, LANES), f32),
             pltpu.VMEM((ROW, 64, LANES), f32),
-            pltpu.VMEM((ROW, 2, 16, LANES), f32),
+            pltpu.VMEM((SLOTS, 4, 16, LANES), f32),
             pltpu.VMEM((ROW, 4, 16, LANES), f32),
             pltpu.VMEM((4, 16, LANES), f32),
             pltpu.VMEM((4, 4, 16, LANES), f32),
@@ -377,17 +375,17 @@
             dma((3,)),
             dma((TILES,)),
             dma,
-            dma((ROW, 3)),
-            dma((3,)),
+            dma((SLOTS,)),
+            dma,
             dma((3,)),
             dma,
             pltpu.SemaphoreType.REGULAR,
         ],
         compiler_params=pltpu.CompilerParams(
-            collective_id=0, has_side_effects=True, vmem_limit_bytes=60 * 1024 * 1024
+            collective_id=0, has_side_effects=True, vmem_limit_bytes=40000 * 1024
         ),
         name="wannier",
-    )(bvectors, jnp.transpose(gshift, (2, 1, 0)), local)
+    )(vectors, shifts, local)
     return result[None]
 
 

time: 75.7 us -> 73.6 us (0.972)
  local copies, waits for them, and re-layouts: 1.57 us -> 0.66 us
    unnamed x1, local copies, waits for them, and re-layouts: 1.57 us -> 0.66 us
where the time goes in v2:
time: 73.6 us; the launch traced here: 73.5 us
  Pallas kernels  72.8 us (99%)
    pallas_call x1, Pallas kernels, per_device(): pl.pallas_call(kernel, out_shape=jax.ShapeDtypeStruct((4, 2, 32, 32), f32...  72.8 us

profile of v2, /device:TPU:1, one launch (start us, length us, event | category | flops | bytes accessed | tf_op | source)
XLA Modules:
  0.0 73.5 jit_solution(14260995626179467078)
XLA Ops:
  0.0 72.8 %wannier.1 = f32[4,2,32,32]{3,2,1,0:T(8,128)S(1)} custom-call(f32[2,3]{1,0:T(2,128)} %bvec_hbm.1, s32[3,2,32]{2,1,0:T(2,128)} %bitcast.7, f32[2,3,32,6400]{3,2,1,0:T(8,128)} %bitcast.6), custom_call_target="tpu_custom_call" | custom-call | tf_op jit(solution)/shard_map/wannier/pallas_call | solution.py:351
  72.8 0.7 copy.5

commit v3 on v2

v3 whole, which is shorter than its diff:
```python
import math

import jax
import jax.numpy as jnp
from jax import lax
from jax.experimental import pallas as pl
from jax.experimental.pallas import tpu as pltpu
from jax.sharding import PartitionSpec as P

GX = 40
GY = 40
NZ = 16
ROW = 8
ROWS = 4
SLOTS = 12
TILES = 6
LANES = 128
EARLY = ((0, 2), (2, 2), (4, 2))
LATE = ((0, 2), (2, 2), (4, 1), (5, 1))
MESH = pl.DeviceIdType.MESH
TWO_PI = 2.0 * math.pi


def split(value):
    high = value.astype(jnp.bfloat16)
    low = (value - high.astype(jnp.float32)).astype(jnp.bfloat16)
    return high, low


def contract(left, right):
    return lax.dot_general(
        left, right, (((1,), (1,)), ((), ())), preferred_element_type=jnp.float32
    )


def kernel(
    bvec_hbm, gshift_hbm, field_ref, out_ref,
    bvec_ref, gshift_ref, buf, xbuf, phase, acc, stage, reduced, total, gathered,
    small_sem, send_sem, early_sem, late_sem, passed_sem, xsend_sem, xrecv_sem, fsend_sem, xfsend_sem,
    rsend_sem, rrecv_sem, gsend_sem, grecv_sem, rows_sem, across_sem,
):
    me = lax.axis_index("ka")
    gx = lax.axis_index("gz")
    row = me // ROW
    own = me % ROW
    zpos = own // 2
    core = own % 2
    side = zpos // 2
    row_up = (row + 1) % ROWS
    row_down = (row + ROWS - 1) % ROWS
    pass_row = jnp.where(core == 0, row_down, row_up)
    pass_from = 8 * core
    pass_to = 8 - 8 * core
    first_k = row * ROW - 4 * core

    def at(r, j):
        return {"ka": r * ROW + j}

    sibling = zpos * 2 + 1 - core
    others = [((zpos + dz) % 4) * 2 for dz in (1, 3, 2)]
    barrier = pltpu.get_barrier_semaphore()
    near = [at(row, z + c) for z in others[:2] for c in range(2)] + [at(row, sibling)]
    near += [at(row_up, own), at(row_down, own)]
    near += [{"gz": (gx + 1) % 4}, {"gz": (gx + 3) % 4}]
    for device in near:
        pl.semaphore_signal(barrier, inc=1, device_id=device, device_id_type=MESH)
    small = [
        pltpu.make_async_copy(bvec_hbm, bvec_ref, small_sem.at[0]),
        pltpu.make_async_copy(gshift_hbm, gshift_ref, small_sem.at[1]),
    ]
    for copy in small:
        copy.start()

    pl.semaphore_wait(barrier, len(near))
    pl.semaphore_signal(across_sem.at[0], inc=1, device_id=at(row, others[1] + core), device_id_type=MESH)
    pl.semaphore_signal(across_sem.at[1], inc=1, device_id={"gz": (gx + 3) % 4}, device_id_type=MESH)

    def extra_source(p):
        comp = jnp.minimum(p // 2, 2)
        start = pl.multiple_of((ROW * TILES + p % 2) * LANES, LANES)
        return field_ref.at[:, comp, :, pl.ds(start, LANES)]

    def lanes_of(block):
        return pl.ds(block[0] * LANES, block[1] * LANES)

    def block_source(p, block):
        start = pl.multiple_of((p * TILES + block[0]) * LANES, LANES)
        return field_ref.at[:, :, :, pl.ds(start, block[1] * LANES)]

    def block_target(slot, block):
        return buf.at[slot, :, :, :, lanes_of(block)]

    def send_extra(z, c):
        pltpu.make_async_remote_copy(
            src_ref=extra_source(z + c), dst_ref=xbuf.at[own + 4 * c],
            send_sem=xsend_sem, recv_sem=xrecv_sem.at[side + c],
            device_id=at(row, z + c), device_id_type=MESH,
        ).start()

    def keep_extra(c):
        pltpu.make_async_copy(
            extra_source(own), xbuf.at[own + 4 * c], xrecv_sem.at[side + c]
        ).start()

    def send_blocks(z, c, blocks, sems):
        for n, block in blocks:
            pltpu.make_async_remote_copy(
                src_ref=block_source(z + c, block), dst_ref=block_target(own + 4 * c, block),
                send_sem=send_sem, recv_sem=sems.at[n],
                device_id=at(row, z + c), device_id_type=MESH,
            ).start()

    def keep_blocks(c, blocks, sems):
        for n, block in blocks:
            pltpu.make_async_copy(
                block_source(own, block), block_target(own + 4 * c, block), sems.at[n]
            ).start()

    early = list(enumerate(EARLY))
    late = list(enumerate(LATE))
    for z in others[:2]:
        send_extra(z, side)
    for z in others[:2]:
        send_blocks(z, side, early[:1], early_sem)
    pl.semaphore_wait(across_sem.at[0], 1)
    send_extra(others[2], side)
    send_blocks(others[2], side, early[:1], early_sem)
    for pair in early[1:]:
        for z in others:
            send_blocks(z, side, [pair], early_sem)
    here = zpos * 2

    @pl.when(core == side)
    def _():
        keep_extra(side)
        keep_blocks(side, early, early_sem)
        send_extra(here, 1 - side)
        send_blocks(here, 1 - side, late, late_sem)

    @pl.when(core != side)
    def _():
        send_extra(here, side)
        send_blocks(here, side, early, early_sem)
        keep_extra(1 - side)
        keep_blocks(1 - side, late, late_sem)

    for pair in late:
        for z in others:
            send_blocks(z, 1 - side, [pair], late_sem)
    for z in others:
        send_extra(z, 1 - side)

    for r in (row_up, row_down):
        pl.semaphore_signal(rows_sem, inc=1, device_id=at(r, own), device_id_type=MESH)

    for copy in small:
        copy.wait()

    row_id = lax.broadcasted_iota(jnp.int32, (16, LANES), 0)
    lane = lax.broadcasted_iota(jnp.int32, (16, TILES * LANES), 1).astype(jnp.float32)
    q = []
    for a in range(3):
        values = jnp.zeros((16, LANES), jnp.float32)
        for d in range(2):
            for i in range(8):
                k = (first_k + i + 32) % 32
                value = bvec_ref[d, a] + gshift_ref[a, d, k].astype(jnp.float32)
                values = jnp.where(row_id == d * 8 + i, value, values)
        q.append(jnp.concatenate([values] * TILES, axis=1))

    def phases_of(start, width):
        cell = lane[:, :width] + start.astype(jnp.float32)
        line = jnp.floor((cell + 0.5) * (1.0 / GX))
        plane = jnp.floor((cell + 0.5) * (1.0 / (GX * GY)))
        xc = cell - GX * line
        yc = line - GY * plane
        zc = plane + (gx * 4).astype(jnp.float32)
        q0, q1, q2 = (values[:, :width] for values in q)
        theta = -TWO_PI * (q0 * xc / GX + q1 * yc / GY + q2 * zc / NZ)
        return jnp.cos(theta), jnp.sin(theta)

    cosine, sine = phases_of(own * TILES * LANES, TILES * LANES)
    phase[0, :, pl.ds(0, TILES * LANES)] = cosine
    phase[1, :, pl.ds(0, TILES * LANES)] = sine
    cosine, sine = phases_of((ROW * TILES + own % 2) * LANES, LANES)
    keep = (own < 6).astype(jnp.float32)
    phase[0, :, pl.ds(TILES * LANES, LANES)] = cosine * keep
    phase[1, :, pl.ds(TILES * LANES, LANES)] = sine * keep
    acc[...] = jnp.zeros_like(acc)

    def wait_block(group, block, sem):
        target = block_target(pl.ds(4 * group, 4), block)
        pltpu.make_async_copy(target, target, sem).wait()

    def wait_extra(group):
        block = xbuf.at[pl.ds(4 * group, 4)]
        pltpu.make_async_copy(block, block, xrecv_sem.at[group]).wait()

    pass_extra = pltpu.make_async_remote_copy(
        src_ref=xbuf.at[pl.ds(pass_from, 4)], dst_ref=xbuf.at[pl.ds(pass_to, 4)],
        send_sem=xfsend_sem, recv_sem=xrecv_sem.at[2 - 2 * core],
        device_id=at(pass_row, own), device_id_type=MESH,
    )

    def pass_block(n, block):
        return pltpu.make_async_remote_copy(
            src_ref=block_target(pl.ds(pass_from, 4), block),
            dst_ref=block_target(pl.ds(pass_to, 4), block),
            send_sem=fsend_sem.at[n], recv_sem=passed_sem.at[n],
            device_id=at(pass_row, own), device_id_type=MESH,
        )

    wait_extra(2 * core)
    pass_extra.start()
    for n, block in early:
        wait_block(2 * core, block, early_sem.at[n])
        pass_block(n, block).start()

    def pair_products(left, rights):
        left_high, left_low = split(left)
        right_high, right_low = split(jnp.concatenate(rights, axis=0))
        return (
            contract(left_high, right_high)
            + contract(left_high, right_low)
            + contract(left_low, right_high)
        )

    def rotate(real, imag, lanes, d, i, comps):
        c = phase[0, pl.ds(d * 8 + i, 1), lanes]
        s = phase[1, pl.ds(d * 8 + i, 1), lanes]
        width = c.shape[1]
        c = jnp.concatenate([jnp.broadcast_to(c, (32, width))] * comps, axis=1)
        s = jnp.concatenate([jnp.broadcast_to(s, (32, width))] * comps, axis=1)
        return [c * real - s * imag, s * real + c * imag]

    def extra_step(i):
        left = xbuf[i].reshape(64, LANES)
        lanes = pl.ds(TILES * LANES, LANES)
        rights = []
        for d, offset in enumerate((1, 4)):
            rights += rotate(xbuf[i + offset, 0], xbuf[i + offset, 1], lanes, d, i, 1)
        acc[i] += pair_products(left, rights)

    def wide(slot, part, lanes):
        return jnp.concatenate([buf[slot, part, comp, :, lanes] for comp in range(3)], axis=1)

    def block_step(i, block):
        lanes = lanes_of(block)
        left = jnp.concatenate([wide(i, 0, lanes), wide(i, 1, lanes)], axis=0)
        rights = []
        for d, offset in enumerate((1, 4)):
            rights += rotate(wide(i + offset, 0, lanes), wide(i + offset, 1, lanes), lanes, d, i, 3)
        acc[i] += pair_products(left, rights)

    lane32 = lax.broadcasted_iota(jnp.int32, (32, LANES), 1)
    lane16 = lax.broadcasted_iota(jnp.int32, (16, LANES), 1)
    holder = core * 4 + zpos
    spans = [(0, 2)] + [(0, 3)] * 3 + [(0, 4)] * 4 + [(2, 2)] + [(3, 1)] * 3

    def target_copy(i):
        part = pl.ds(*spans[i])
        target = (first_k + i + 32) % 32
        return target, pltpu.make_async_remote_copy(
            src_ref=stage.at[i, part], dst_ref=reduced.at[holder, part],
            send_sem=rsend_sem.at[i], recv_sem=rrecv_sem,
            device_id={"ka": target}, device_id_type=MESH,
        )

    def send_target(i):
        part = pl.ds(*spans[i])
        target, copy = target_copy(i)

        @pl.when(target == me)
        def _():
            pltpu.make_async_copy(stage.at[i, part], reduced.at[holder, part], rrecv_sem).start()

        @pl.when(target != me)
        def _():
            copy.start()

    def finish_matrices(i):
        top = acc[i, pl.ds(0, 32), :]
        bottom = acc[i, pl.ds(32, 32), :]
        swapped = jnp.where(
            lane32 % 64 < 32, pltpu.roll(bottom, 96, 1), -pltpu.roll(bottom, 32, 1)
        )
        value = top + swapped
        turned = pltpu.roll(value, 64, 1)
        along_x = jnp.where(lane16 < 64, value[:16], turned[16:])
        along_y = jnp.where(lane16 < 64, turned[:16], value[16:])
        stage[i, 0] = along_x
        stage[i, 1] = along_y
        stage[i + 1, 2] = along_x
        stage[i + 4, 3] = along_y

    for n, block in late:
        for e, other in early:
            if block[0] <= other[0] < block[0] + block[1]:
                wait_block(2 - 2 * core, other, passed_sem.at[e])
        wait_block(1, block, late_sem.at[n])
        for i in range(ROW):
            block_step(i, block)
    pl.semaphore_wait(across_sem.at[1], 1)
    pl.semaphore_wait(rows_sem, 2)
    wait_extra(2 - 2 * core)
    wait_extra(1)
    for i in range(ROW):
        extra_step(i)
        finish_matrices(i)
    for i in range(SLOTS):
        send_target(i)

    def slab_copy(dx):
        return pltpu.make_async_remote_copy(
            src_ref=total, dst_ref=gathered.at[gx],
            send_sem=gsend_sem.at[dx - 1], recv_sem=grecv_sem,
            device_id={"gz": (gx + dx) % 4}, device_id_type=MESH,
        )

    pltpu.make_async_copy(reduced, reduced, rrecv_sem).wait()
    value = reduced[0]
    for j in range(1, ROW):
        value = value + reduced[j]
    total[...] = value
    for dx in (2, 1, 3):
        slab_copy(dx).start()
    gathered[gx] = value

    seven = xbuf.at[pl.ds(0, 7)]
    pltpu.make_async_copy(seven, seven, xsend_sem).wait()
    pass_extra.wait_send()

    sent = buf.at[pl.ds(0, 7)]
    pltpu.make_async_copy(sent, sent, send_sem).wait()
    for n, block in early:
        pass_block(n, block).wait_send()
    for i in range(SLOTS):
        target, copy = target_copy(i)

        @pl.when(target != me)
        def _():
            copy.wait_send()

    block = gathered.at[pl.ds(0, 3)]
    pltpu.make_async_copy(block, block, grecv_sem).wait()
    summed = gathered[0] + gathered[1] + gathered[2] + gathered[3]
    for index, direction in ((0, 0), (1, 2), (2, 1), (3, 3)):
        value = summed[index]
        real = jnp.concatenate([value[:, 0:32], value[:, 64:96]], axis=0)
        imag = jnp.concatenate([value[:, 32:64], value[:, 96:128]], axis=0)
        if index < 2:
            out_ref[direction, 0] = real
            out_ref[direction, 1] = imag
        else:
            out_ref[direction, 0] = real.T
            out_ref[direction, 1] = -imag.T
    for dx in (1, 2, 3):
        slab_copy(dx).wait_send()


def per_device(fields, bvectors, gshift):
    local, vectors, shifts = (
        pltpu.with_memory_space_constraint(value, pltpu.HBM)
        for value in (
            jnp.transpose(fields[0], (0, 2, 1, 3)), bvectors, jnp.transpose(gshift, (2, 1, 0))
        )
    )
    dma = pltpu.SemaphoreType.DMA
    f32 = jnp.float32
    result = pl.pallas_call(
        kernel,
        out_shape=jax.ShapeDtypeStruct((4, 2, 32, 32), f32),
        in_specs=[
            pl.BlockSpec(memory_space=pltpu.HBM),
            pl.BlockSpec(memory_space=pltpu.HBM),
            pl.BlockSpec(memory_space=pltpu.HBM),
        ],
        out_specs=pl.BlockSpec(memory_space=pltpu.VMEM),
        scratch_shapes=[
            pltpu.SMEM((2, 3), f32),
            pltpu.SMEM((3, 2, 32), jnp.int32),
            pltpu.VMEM((SLOTS, 2, 3, 32, TILES * LANES), f32),
            pltpu.VMEM((SLOTS, 2, 32, LANES), f32),
            pltpu.VMEM((2, 16, (TILES + 1) * LANES), f32),
            pltpu.VMEM((ROW, 64, LANES), f32),
            pltpu.VMEM((SLOTS, 4, 16, LANES), f32),
            pltpu.VMEM((ROW, 4, 16, LANES), f32),
            pltpu.VMEM((4, 16, LANES), f32),
            pltpu.VMEM((4, 4, 16, LANES), f32),
            dma((2,)),
            dma,
            dma((len(EARLY),)),
            dma((len(LATE),)),
            dma((len(EARLY),)),
            dma,
            dma((3,)),
            dma((len(EARLY),)),
            dma,
            dma((SLOTS,)),
            dma,
            dma((3,)),
            dma,
            pltpu.SemaphoreType.REGULAR,
            pltpu.SemaphoreType.REGULAR((2,)),
        ],
        compiler_params=pltpu.CompilerParams(
            collective_id=0, has_side_effects=True, vmem_limit_bytes=40000 * 1024
        ),
        name="wannier",
    )(vectors, shifts, local)
    return result[None]


def solution(mesh):
    in_specs = (P("ka", None, None, None, "gz"), P(), P())
    out_specs = P("ka", None, None, None, None)
    return jax.shard_map(
        per_device, mesh=mesh, in_specs=in_specs, out_specs=out_specs, check_vma=False
    )
```

time: 73.6 us -> 72.9 us (level)
  no operation moved by 1% of the time
where the time goes in v3:
time: 72.9 us; the launch traced here: 72.8 us
  Pallas kernels  72.2 us (99%)
    pallas_call x1, Pallas kernels, per_device(): pl.pallas_call(kernel, out_shape=jax.ShapeDtypeStruct((4, 2, 32, 32), f32...  72.2 us

profile of v3, /device:TPU:1, one launch (start us, length us, event | category | flops | bytes accessed | tf_op | source)
XLA Modules:
  0.0 72.8 jit_solution(18370189227572701571)
XLA Ops:
  0.0 72.2 %wannier.1 = f32[4,2,32,32]{3,2,1,0:T(8,128)S(1)} custom-call(f32[2,3]{1,0:T(2,128)} %bvec_hbm.1, s32[3,2,32]{2,1,0:T(2,128)} %bitcast.7, f32[2,3,32,6400]{3,2,1,0:T(8,128)} %bitcast.6), custom_call_target="tpu_custom_call" | custom-call | tf_op jit(solution)/shard_map/wannier/pallas_call | solution.py:370
  72.2 0.7 copy.5

commit v4 on v3

--- a/solution.py
+++ b/solution.py
@@ -35,8 +35,8 @@
 
 def kernel(
     bvec_hbm, gshift_hbm, field_ref, out_ref,
-    bvec_ref, gshift_ref, buf, xbuf, phase, acc, stage, reduced, total, gathered,
-    small_sem, send_sem, early_sem, late_sem, passed_sem, xsend_sem, xrecv_sem, fsend_sem, xfsend_sem,
+    bvec_ref, gshift_ref, local, buf, xbuf, phase, acc, stage, reduced, total, gathered,
+    small_sem, load_sem, send_sem, early_sem, late_sem, passed_sem, xsend_sem, xrecv_sem, fsend_sem, xfsend_sem,
     rsend_sem, rrecv_sem, gsend_sem, grecv_sem, rows_sem, across_sem,
 ):
     me = lax.axis_index("ka")
@@ -71,41 +71,57 @@
     for copy in small:
         copy.start()
 
+
+    def load(p):
+        part = pl.ds(pl.multiple_of(p * TILES * LANES, LANES), TILES * LANES)
+        return pltpu.make_async_copy(
+            field_ref.at[:, :, :, part], local.at[:, :, :, part], load_sem.at[p]
+        )
+
+    odd = pl.ds(ROW * TILES * LANES, 2 * LANES)
+    load_odd = pltpu.make_async_copy(
+        field_ref.at[:, :, :, odd], local.at[:, :, :, odd], load_sem.at[ROW]
+    )
+    load_odd.start()
+    for c in (side, 1 - side):
+        for z in others:
+            load(z + c).start()
+    load(sibling).start()
     pl.semaphore_wait(barrier, len(near))
     pl.semaphore_signal(across_sem.at[0], inc=1, device_id=at(row, others[1] + core), device_id_type=MESH)
     pl.semaphore_signal(across_sem.at[1], inc=1, device_id={"gz": (gx + 3) % 4}, device_id_type=MESH)
 
-    def extra_source(p):
+    def extra_source(source, p):
         comp = jnp.minimum(p // 2, 2)
         start = pl.multiple_of((ROW * TILES + p % 2) * LANES, LANES)
-        return field_ref.at[:, comp, :, pl.ds(start, LANES)]
+        return source.at[:, comp, :, pl.ds(start, LANES)]
 
     def lanes_of(block):
         return pl.ds(block[0] * LANES, block[1] * LANES)
 
-    def block_source(p, block):
+    def block_source(source, p, block):
         start = pl.multiple_of((p * TILES + block[0]) * LANES, LANES)
-        return field_ref.at[:, :, :, pl.ds(start, block[1] * LANES)]
+        return source.at[:, :, :, pl.ds(start, block[1] * LANES)]
 
     def block_target(slot, block):
         return buf.at[slot, :, :, :, lanes_of(block)]
 
     def send_extra(z, c):
         pltpu.make_async_remote_copy(
-            src_ref=extra_source(z + c), dst_ref=xbuf.at[own + 4 * c],
+            src_ref=extra_source(local, z + c), dst_ref=xbuf.at[own + 4 * c],
             send_sem=xsend_sem, recv_sem=xrecv_sem.at[side + c],
             device_id=at(row, z + c), device_id_type=MESH,
         ).start()
 
     def keep_extra(c):
         pltpu.make_async_copy(
-            extra_source(own), xbuf.at[own + 4 * c], xrecv_sem.at[side + c]
+            extra_source(field_ref, own), xbuf.at[own + 4 * c], xrecv_sem.at[side + c]
         ).start()
 
     def send_blocks(z, c, blocks, sems):
         for n, block in blocks:
             pltpu.make_async_remote_copy(
-                src_ref=block_source(z + c, block), dst_ref=block_target(own + 4 * c, block),
+                src_ref=block_source(local, z + c, block), dst_ref=block_target(own + 4 * c, block),
                 send_sem=send_sem, recv_sem=sems.at[n],
                 device_id=at(row, z + c), device_id_type=MESH,
             ).start()
@@ -113,15 +129,18 @@
     def keep_blocks(c, blocks, sems):
         for n, block in blocks:
             pltpu.make_async_copy(
-                block_source(own, block), block_target(own + 4 * c, block), sems.at[n]
+                block_source(field_ref, own, block), block_target(own + 4 * c, block), sems.at[n]
             ).start()
 
     early = list(enumerate(EARLY))
     late = list(enumerate(LATE))
     for z in others[:2]:
+        load(z + side).wait()
+        send_blocks(z, side, early[:1], early_sem)
+    load_odd.wait()
+    for z in others[:2]:
         send_extra(z, side)
-    for z in others[:2]:
-        send_blocks(z, side, early[:1], early_sem)
+    load(others[2] + side).wait()
     pl.semaphore_wait(across_sem.at[0], 1)
     send_extra(others[2], side)
     send_blocks(others[2], side, early[:1], early_sem)
@@ -129,6 +148,7 @@
         for z in others:
             send_blocks(z, side, [pair], early_sem)
     here = zpos * 2
+    load(sibling).wait()
 
     @pl.when(core == side)
     def _():
@@ -144,6 +164,8 @@
         keep_extra(1 - side)
         keep_blocks(1 - side, late, late_sem)
 
+    for z in others:
+        load(z + 1 - side).wait()
     for pair in late:
         for z in others:
             send_blocks(z, 1 - side, [pair], late_sem)
@@ -379,6 +401,7 @@
         scratch_shapes=[
             pltpu.SMEM((2, 3), f32),
             pltpu.SMEM((3, 2, 32), jnp.int32),
+            pltpu.VMEM((2, 3, 32, GX * GY * NZ // 4), f32),
             pltpu.VMEM((SLOTS, 2, 3, 32, TILES * LANES), f32),
             pltpu.VMEM((SLOTS, 2, 32, LANES), f32),
             pltpu.VMEM((2, 16, (TILES + 1) * LANES), f32),
@@ -388,6 +411,7 @@
             pltpu.VMEM((4, 16, LANES), f32),
             pltpu.VMEM((4, 4, 16, LANES), f32),
             dma((2,)),
+            dma((ROW + 1,)),
             dma,
             dma((len(EARLY),)),
             dma((len(LATE),)),

time: 72.9 us -> 72.8 us (level)
  no operation moved by 1% of the time
where the time goes in v4:
time: 72.8 us; the launch traced here: 72.7 us
  Pallas kernels  72 us (99%)
    pallas_call x1, Pallas kernels, per_device(): pl.pallas_call(kernel, out_shape=jax.ShapeDtypeStruct((4, 2, 32, 32), f32...  72 us

profile of v4, /device:TPU:1, one launch (start us, length us, event | category | flops | bytes accessed | tf_op | source)
XLA Modules:
  0.0 72.7 jit_solution(3480751183098505604)
XLA Ops:
  0.0 72.0 %wannier.1 = f32[4,2,32,32]{3,2,1,0:T(8,128)S(1)} custom-call(f32[2,3]{1,0:T(2,128)} %bvec_hbm.1, s32[3,2,32]{2,1,0:T(2,128)} %bitcast.7, f32[2,3,32,6400]{3,2,1,0:T(8,128)} %bitcast.6), custom_call_target="tpu_custom_call" | custom-call | tf_op jit(solution)/shard_map/wannier/pallas_call | solution.py:392
  72.0 0.7 copy.5

commit v5 on v3

--- a/solution.py
+++ b/solution.py
@@ -219,11 +219,11 @@
     def pair_products(left, rights):
         left_high, left_low = split(left)
         right_high, right_low = split(jnp.concatenate(rights, axis=0))
-        return (
-            contract(left_high, right_high)
-            + contract(left_high, right_low)
-            + contract(left_low, right_high)
-        )
+        both = contract(
+            jnp.concatenate([left_high, left_low], axis=0),
+            jnp.concatenate([right_high, right_low], axis=0),
+        )
+        return both[:64, :128] + both[64:, :128] + both[:64, 128:]
 
     def rotate(real, imag, lanes, d, i, comps):
         c = phase[0, pl.ds(d * 8 + i, 1), lanes]

time: 72.9 us -> 72.2 us (level)
  no operation moved by 1% of the time
where the time goes in v5:
time: 72.2 us
  Pallas kernels  71.5 us (99%)
    pallas_call x1, Pallas kernels, per_device(): pl.pallas_call(kernel, out_shape=jax.ShapeDtypeStruct((4, 2, 32, 32), f32...  71.5 us

profile of v5, /device:TPU:1, one launch (start us, length us, event | category | flops | bytes accessed | tf_op | source)
XLA Modules:
  0.0 72.2 jit_solution(14946203992258286726)
XLA Ops:
  0.0 71.5 %wannier.1 = f32[4,2,32,32]{3,2,1,0:T(8,128)S(1)} custom-call(f32[2,3]{1,0:T(2,128)} %bvec_hbm.1, s32[3,2,32]{2,1,0:T(2,128)} %bitcast.7, f32[2,3,32,6400]{3,2,1,0:T(8,128)} %bitcast.6), custom_call_target="tpu_custom_call" | custom-call | tf_op jit(solution)/shard_map/wannier/pallas_call | solution.py:370
  71.5 0.7 copy.5

commit v6 on v5

--- a/solution.py
+++ b/solution.py
@@ -15,8 +15,8 @@
 SLOTS = 12
 TILES = 6
 LANES = 128
-EARLY = ((0, 2), (2, 2), (4, 2))
-LATE = ((0, 2), (2, 2), (4, 1), (5, 1))
+EARLY = ((0, 3), (3, 3))
+LATE = ((0, 3), (3, 2), (5, 1))
 MESH = pl.DeviceIdType.MESH
 TWO_PI = 2.0 * math.pi
 
@@ -270,13 +270,10 @@
         part = pl.ds(*spans[i])
         target, copy = target_copy(i)
 
-        @pl.when(target == me)
-        def _():
+        def stay():
             pltpu.make_async_copy(stage.at[i, part], reduced.at[holder, part], rrecv_sem).start()
 
-        @pl.when(target != me)
-        def _():
-            copy.start()
+        lax.cond(target == me, stay, copy.start)
 
     def finish_matrices(i):
         top = acc[i, pl.ds(0, 32), :]

time: 72.2 us -> 72.2 us (level)
  no operation moved by 1% of the time
where the time goes in v6:
time: 72.2 us; the launch traced here: 72.1 us
  Pallas kernels  71.4 us (99%)
    pallas_call x1, Pallas kernels, per_device(): pl.pallas_call(kernel, out_shape=jax.ShapeDtypeStruct((4, 2, 32, 32), f32...  71.4 us

profile of v6, /device:TPU:1, one launch (start us, length us, event | category | flops | bytes accessed | tf_op | source)
XLA Modules:
  0.0 72.1 jit_solution(15015690828111159695)
XLA Ops:
  0.0 71.4 %wannier.1 = f32[4,2,32,32]{3,2,1,0:T(8,128)S(1)} custom-call(f32[2,3]{1,0:T(2,128)} %bvec_hbm.1, s32[3,2,32]{2,1,0:T(2,128)} %bitcast.7, f32[2,3,32,6400]{3,2,1,0:T(8,128)} %bitcast.6), custom_call_target="tpu_custom_call" | custom-call | tf_op jit(solution)/shard_map/wannier/pallas_call | solution.py:367
  71.4 0.7 copy.5

commit v7 on v6

--- a/solution.py
+++ b/solution.py
@@ -239,7 +239,7 @@
         rights = []
         for d, offset in enumerate((1, 4)):
             rights += rotate(xbuf[i + offset, 0], xbuf[i + offset, 1], lanes, d, i, 1)
-        acc[i] += pair_products(left, rights)
+        return pair_products(left, rights)
 
     def wide(slot, part, lanes):
         return jnp.concatenate([buf[slot, part, comp, :, lanes] for comp in range(3)], axis=1)
@@ -275,9 +275,8 @@
 
         lax.cond(target == me, stay, copy.start)
 
-    def finish_matrices(i):
-        top = acc[i, pl.ds(0, 32), :]
-        bottom = acc[i, pl.ds(32, 32), :]
+    def finish_matrices(i, products):
+        top, bottom = products[:32], products[32:]
         swapped = jnp.where(
             lane32 % 64 < 32, pltpu.roll(bottom, 96, 1), -pltpu.roll(bottom, 32, 1)
         )
@@ -302,8 +301,7 @@
     wait_extra(2 - 2 * core)
     wait_extra(1)
     for i in range(ROW):
-        extra_step(i)
-        finish_matrices(i)
+        finish_matrices(i, acc[i] + extra_step(i))
     for i in range(SLOTS):
         send_target(i)
 

time: 72.2 us -> 72.2 us (level)
  no operation moved by 1% of the time
where the time goes in v7:
time: 72.2 us; the launch traced here: 72.1 us
  Pallas kernels  71.4 us (99%)
    pallas_call x1, Pallas kernels, per_device(): pl.pallas_call(kernel, out_shape=jax.ShapeDtypeStruct((4, 2, 32, 32), f32...  71.4 us

profile of v7, /device:TPU:1, one launch (start us, length us, event | category | flops | bytes accessed | tf_op | source)
XLA Modules:
  0.0 72.1 jit_solution(15015690828111159695)
XLA Ops:
  0.0 71.4 %wannier.1 = f32[4,2,32,32]{3,2,1,0:T(8,128)S(1)} custom-call(f32[2,3]{1,0:T(2,128)} %bvec_hbm.1, s32[3,2,32]{2,1,0:T(2,128)} %bitcast.7, f32[2,3,32,6400]{3,2,1,0:T(8,128)} %bitcast.6), custom_call_target="tpu_custom_call" | custom-call | tf_op jit(solution)/shard_map/wannier/pallas_call | solution.py:365
  71.4 0.7 copy.5
